TPU v7x, 512 devices: a whole 4x4x16 slice. The times are simulated.
512 devices in a mesh: dp: 4 (over y), expert: 128 (over x, z, core).
Axes of the slice: x: 4, y: 4, z: 16, core: 2. Of those that a mesh axis runs over, the one named last changes fastest.
Arguments:
- slot_grads: bfloat16 [4, 128, 384, 2048], P('dp', 'expert'), may hold values from -0.23925781 to 0.23925781
- momentum: float32 [384, 64, 2048], P('expert', None, 'dp'), may hold values from -0.16 to 0.16
- master_weights: float32 [384, 64, 2048], P('expert', None, 'dp'), may hold values from -0.3125 to 0.3125
- current_slots: int32 [128, 1], replicated, may hold values from 0 to 63
- next_slots: int32 [128, 1], replicated, may hold values from 0 to 63
- live_counts: int32 [4, 128], P('dp', 'expert'), may hold values from 1 to 512
- route_index: int32 [4, 128, 4, 128], P('dp', 'expert'), may hold values from 0 to 127, each once within a row
- activations: bfloat16 [4, 128, 512, 384], P('dp', 'expert'), may hold values from -6 to 6
Outputs:
- new_momentum: float32 [384, 64, 2048], P('expert', None, 'dp')
- expert_out: bfloat16 [4, 128, 512, 2048], P('dp', 'expert')
Inputs may be any that keep to these rules, and one draw needn't show every extreme that they name: `current_slots`: every expert is held by at least one slot. `next_slots`: every expert is held by at least one slot. `route_index`: each block of 128 indices names every row of its block once.
All inputs are finite; a program needn't handle non-finite values.
Results may differ from a plain program's by a relative error of at most 0.015.
Values may be sent and summed in bfloat16 or wider, within the bound.
A program may use at most 64 MiB of HBM per device.

v0:
```python
import jax
import jax.numpy as jnp
from jax import lax
from jax.sharding import PartitionSpec as P

QBLOCK = 128


momentum_decay = 0.9
step_rate = 0.5
epsilon = 1e-06
range_limit = 448.0


def cut_along(x, dim, peers):
    shape = x.shape
    parts = x.reshape(*shape[:dim], peers, shape[dim] // peers, *shape[dim + 1 :])
    return jnp.moveaxis(parts, dim, 0)


def sent_and_summed(x, axis, dim):
    parts = cut_along(x, dim, lax.axis_size(axis))
    arrived = lax.all_to_all(parts, axis, split_axis=0, concat_axis=0, tiled=True)
    return arrived.astype(jnp.float32).sum(axis=0)


def sent_together(arrays, axis, split_dim, concat_dim, along):
    ends, at = ([], 0)
    for a in arrays[:-1]:
        at += a.shape[along]
        ends.append(at)
    both = jnp.concatenate(arrays, axis=along)
    return tuple(
        jnp.split(
            lax.all_to_all(both, axis, split_axis=split_dim, concat_axis=concat_dim, tiled=True),
            ends,
            axis=along,
        )
    )


def joined_along(parts, dim):
    parts = jnp.moveaxis(parts, 0, dim)
    shape = parts.shape
    return parts.reshape(*shape[:dim], shape[dim] * shape[dim + 1], *shape[dim + 2 :])


def copy_for_each(x, axis):
    copies = jnp.broadcast_to(x, (lax.axis_size(axis), *x.shape))
    return lax.all_to_all(copies, axis, split_axis=0, concat_axis=0, tiled=True)


def gathered_copies(x, axis, dim):
    return joined_along(copy_for_each(x, axis), dim)


def select_rows(activations, route_index):
    block_count = route_index.shape[2]
    block_rows = route_index.shape[3]
    hidden_rows = activations.shape[3]
    blocked = activations[0, 0].reshape(block_count, block_rows, hidden_rows)
    picked = jnp.take_along_axis(blocked, route_index[0, 0][:, :, None], axis=1)
    return picked.reshape(block_count * block_rows, hidden_rows)


def dequantize(values, scales):
    hidden_rows, columns = values.shape
    expanded = values.reshape(hidden_rows, columns // QBLOCK, QBLOCK).astype(jnp.float32)
    expanded = expanded * scales.astype(jnp.float32)[:, :, None]
    return expanded.reshape(hidden_rows, columns).astype(jnp.bfloat16)


def shards(
    slot_grads,
    momentum,
    master_weights,
    current_slots,
    next_slots,
    live_counts,
    route_index,
    activations,
):
    expert_count = lax.axis_size("expert")
    gradient = slot_grads[0, 0]
    hidden_rows = gradient.shape[0]
    slice_rows = hidden_rows // expert_count
    experts = momentum.shape[1]
    columns = momentum.shape[2]
    labels = jnp.arange(experts, dtype=jnp.int32)
    owner_table = current_slots[:, 0][None, :] == labels[:, None]
    summed = sent_and_summed(gradient.astype(jnp.float32).astype(jnp.bfloat16), "dp", 1)
    pieces = summed.reshape(expert_count, slice_rows, columns)
    received = lax.all_to_all(
        pieces.astype(jnp.bfloat16), "expert", split_axis=0, concat_axis=0, tiled=True
    ).astype(pieces.dtype)
    totals = jnp.einsum(
        "xs,spk->pxk", owner_table.astype(jnp.float32), received, precision=lax.Precision.HIGHEST
    )
    new_momentum = momentum_decay * momentum + totals
    weights = master_weights - step_rate * new_momentum
    blocks = weights.reshape(slice_rows, experts, columns // QBLOCK, QBLOCK)
    previous = master_weights.reshape(slice_rows, experts, columns // QBLOCK, QBLOCK)
    scales = (jnp.max(jnp.abs(previous), axis=3) / range_limit + epsilon).astype(jnp.bfloat16)
    scaled = blocks / scales.astype(jnp.float32)[:, :, :, None]
    quantized = jnp.clip(scaled, -range_limit, range_limit).astype(jnp.bfloat16)
    quantized = quantized.reshape(slice_rows, experts, columns)
    chooser = (next_slots[:, 0][:, None] == labels[None, :]).astype(jnp.bfloat16)
    selected = select_rows(activations, route_index)
    sent_values = jnp.einsum(
        "sx,pxk->spk", chooser, quantized, preferred_element_type=jnp.float32
    ).astype(jnp.bfloat16)
    sent_scales = jnp.einsum(
        "sx,pxb->spb", chooser, scales, preferred_element_type=jnp.float32
    ).astype(jnp.bfloat16)
    got_values, got_scales = sent_together((sent_values, sent_scales), "expert", 0, 0, 2)
    weight_cols = dequantize(
        got_values.reshape(hidden_rows, columns), got_scales.reshape(hidden_rows, columns // QBLOCK)
    )
    product = jnp.dot(
        selected, gathered_copies(weight_cols, "dp", 1), preferred_element_type=jnp.float32
    )
    live = jnp.arange(product.shape[0], dtype=jnp.int32) < live_counts[0, 0]
    expert_out = jnp.where(live[:, None], product, 0.0).astype(jnp.bfloat16)
    return (new_momentum, expert_out[None, None])


def solution(mesh):
    in_specs = (
        P("dp", "expert", None, None),
        P("expert", None, "dp"),
        P("expert", None, "dp"),
        P(),
        P(),
        P("dp", "expert"),
        P("dp", "expert", None, None),
        P("dp", "expert", None, None),
    )
    out_specs = (P("expert", None, "dp"), P("dp", "expert", None, None))
    return jax.shard_map(shards, mesh=mesh, in_specs=in_specs, out_specs=out_specs, check_vma=False)
```

profile of v0, /device:TPU:6, one launch (start us, length us, event | category | flops | bytes accessed | tf_op | source)
XLA Modules:
  0.0 157.7 jit_solution(5091341392820254929)
XLA Ops:
  0.6 1.9 %copy.35 = bf16[1,1,384,2048]{2,3,1,0:T(8,128)(2,1)S(1)} copy(bf16[1,1,384,2048]{3,2,1,0:T(8,128)(2,1)} %param.8) | data formatting | bytes 3145728 | tf_op args[0]
  2.6 0.8 copy.36
  3.3 25.0 %all_to_all.20 = bf16[4,384,512]{2,1,0:T(8,128)(2,1)S(1)} all-to-all(bf16[4,384,512]{2,1,0:T(8,128)(2,1)S(1)} %copy.36), channel_id=1, replica_groups=mesh['dp'=4,'expert'=128] {'dp'}, dimensions={0} | all-to-all | bytes 3145728 | tf_op jit(solution)/shard_map/all_to_all | solution.py:23
  28.3 0.4 reduce_sum.12
  28.8 1.0 convert_element_type.57
  29.8 20.0 %all-to-all-start.1 = ((bf16[128,3,512]{2,1,0:T(4,128)(2,1)}), bf16[128,3,512]{2,1,0:T(4,128)(2,1)S(1)}, u32[]{:S(2)}, u32[]{:S(2)}) async-start(bf16[128,3,512]{2,1,0:T(4,128)(2,1)} %convert_element_type.57), calls=%async_computation.1 | async-start | bytes 1048576 | tf_op jit(solution)/shard_map/all_to_all | solution.py:93
  49.9 0.1 abs.7
  50.0 0.3 reduce_max.9
  50.4 0.1 copy.39
  50.6 0.1 convolution_convert_fusion.1
  50.7 0.2 copy.40
  50.9 0.3 div.19
  51.2 0.2 div.20
  51.3 30.6 %all-to-all-done.1 = bf16[128,3,512]{2,1,0:T(4,128)(2,1)S(1)} async-done(((bf16[128,3,512]{2,1,0:T(4,128)(2,1)}), bf16[128,3,512]{2,1,0:T(4,128)(2,1)S(1)}, u32[]{:S(2)}, u32[]{:S(2)}) %all-to-all-start.1) | async-done | bytes 393248 | tf_op jit(solution)/shard_map/all_to_all | solution.py:93
  81.9 0.2 fusion.1
  82.1 0.3 convolution_convert_fusion
  82.5 0.4 copy.41
  82.9 45.6 %all_to_all.21 = bf16[128,3,516]{2,1,0:T(4,128)(2,1)S(1)} all-to-all(bf16[128,3,516]{2,1,0:T(4,128)(2,1)S(1)} %copy.41), channel_id=1, replica_groups=mesh['dp'=4,'expert'=128] {'expert'}, dimensions={0} | all-to-all | bytes 792576 | tf_op jit(solution)/shard_map/all_to_all | solution.py:35
  128.6 0.1 copy.48
  128.7 0.2 copy.46
  128.9 0.1 reshape.133
  129.0 0.1 slice_convert_fusion
  129.1 0.4 reshape.123
  129.5 0.5 mul.27
  130.0 0.2 fusion.2
  130.2 0.2 copy.45
  130.4 1.3 broadcast_in_dim.34
  131.7 3.7 %all-to-all-start.3 = ((bf16[4,384,512]{1,2,0:T(8,128)(2,1)}), bf16[4,384,512]{1,2,0:T(8,128)(2,1)S(1)}, u32[]{:S(2)}, u32[]{:S(2)}) async-start(bf16[4,384,512]{1,2,0:T(8,128)(2,1)} %broadcast_in_dim.34), calls=%async_computation.3 | async-start | bytes 3145728 | tf_op jit(solution)/shard_map/all_to_all | solution.py:50
  136.1 3.7 %gather_fusion = bf16[512,384]{1,0:T(8,128)(2,1)S(1)} fusion(bf16[4,128,384]{2,1,0:T(8,128)(2,1)S(1)} %bitcast.41, s32[512]{0:T(512)S(1)} %fusion.15), kind=kCustom, calls=%fused_computation | custom fusion | bytes 790528 | tf_op jit(solution)/shard_map/jit(take_along_axis)/gather | solution.py:62
  139.8 0.1 broadcast_select_fusion
  139.9 15.2 %all-to-all-done.3 = bf16[4,384,512]{1,2,0:T(8,128)(2,1)S(1)} async-done(((bf16[4,384,512]{1,2,0:T(8,128)(2,1)}), bf16[4,384,512]{1,2,0:T(8,128)(2,1)S(1)}, u32[]{:S(2)}, u32[]{:S(2)}) %all-to-all-start.3) | async-done | bytes 1572896 | tf_op jit(solution)/shard_map/all_to_all | solution.py:50
  155.1 2.6 %fusion = bf16[1,1,512,2048]{3,2,1,0:T(8,128)(2,1)} fusion(bf16[512,384]{1,0:T(8,128)(2,1)S(1)} %bitcast.46, bf16[384,2048]{0,1:T(8,128)(2,1)S(1)} %bitcast.44, pred[512]{0:T(512)(128)(4,1)S(1)} %iota_compare_fusion.2), kind=kOutput, calls=%fused_computation.2 | convolution fusion | flops 807403520 | bytes 4063744 | tf_op jit(solution)/shard_map/dot_general | solution.py:119
  (22 shorter events, 0.3 us)
Async XLA Ops:
  0.6 135.4 %copy-start = (bf16[1,1,512,384]{3,2,1,0:T(8,128)(2,1)S(1)}, bf16[1,1,512,384]{3,2,1,0:T(8,128)(2,1)}, u32[]{:S(2)}) copy-start(bf16[1,1,512,384]{3,2,1,0:T(8,128)(2,1)} %param.15) | copy-start | bytes 1179652
  28.3 21.5 %copy-start.1 = (f32[3,64,512]{2,1,0:T(8,128)S(1)}, f32[3,64,512]{2,1,0:T(8,128)}, u32[]{:S(2)}) copy-start(f32[3,64,512]{2,1,0:T(8,128)} %param.10) | copy-start | bytes 1179652
  29.8 20.8 %copy-start.6 = (s32[128,1]{0,1:T(1,128)S(1)}, s32[128,1]{0,1:T(1,128)}, u32[]{:S(2)}) copy-start(s32[128,1]{0,1:T(1,128)} %param.12) | copy-start | bytes 1540
  29.8 52.1 %all-to-all-start.1 = ((bf16[128,3,512]{2,1,0:T(4,128)(2,1)}), bf16[128,3,512]{2,1,0:T(4,128)(2,1)S(1)}, u32[]{:S(2)}, u32[]{:S(2)}) async-start(bf16[128,3,512]{2,1,0:T(4,128)(2,1)} %convert_element_type.57), calls=%async_computation.1 | async-start | bytes 1048576 | tf_op jit(solution)/shard_map/all_to_all | solution.py:93
  49.9 32.0 %copy-start.2 = (f32[3,64,512]{2,1,0:T(8,128)S(1)}, f32[3,64,512]{2,1,0:T(8,128)}, u32[]{:S(2)}) copy-start(f32[3,64,512]{2,1,0:T(8,128)} %param.9) | copy-start | bytes 1179652
  49.9 32.0 %copy-start.5 = (s32[128,1]{0,1:T(1,128)S(1)}, s32[128,1]{0,1:T(1,128)}, u32[]{:S(2)}) copy-start(s32[128,1]{0,1:T(1,128)} %param.11) | copy-start | bytes 1540
  82.1 0.8 copy-start.3
  131.7 4.4 %copy-start.4 = (s32[1,1,4,128]{3,2,1,0:T(4,128)S(1)}, s32[1,1,4,128]{3,2,1,0:T(4,128)}, u32[]{:S(2)}) copy-start(s32[1,1,4,128]{3,2,1,0:T(4,128)} %param.14) | copy-start | bytes 6148
  131.7 23.4 %all-to-all-start.3 = ((bf16[4,384,512]{1,2,0:T(8,128)(2,1)}), bf16[4,384,512]{1,2,0:T(8,128)(2,1)S(1)}, u32[]{:S(2)}, u32[]{:S(2)}) async-start(bf16[4,384,512]{1,2,0:T(8,128)(2,1)} %broadcast_in_dim.34), calls=%async_computation.3 | async-start | bytes 3145728 | tf_op jit(solution)/shard_map/all_to_all | solution.py:50
where the time goes:
time: 160 us; the launch traced here: 158 us
  blocking collectives  70.6 us (44%)
  waiting for transfers between devices  45.8 us (29%)
  starting transfers between devices  23.7 us (15%)
  local copies, waits for them, and re-layouts  11.6 us (7%)
  matrix products  3.26 us (2%)
    all_to_all x1, blocking collectives, sent_together(): lax.all_to_all(both, axis, split_axis=split_dim, concat_axis=concat_dim,...  45.6 us
    all_to_all x1, waiting for transfers between devices, shards(): lax.all_to_all(pieces.astype(jnp.bfloat16), 'expert', split_axis=0, conca...  30.6 us
    all_to_all x1, blocking collectives, sent_and_summed(): lax.all_to_all(parts, axis, split_axis=0, concat_axis=0, tiled=True)  25 us
    all_to_all x1, starting transfers between devices, shards(): lax.all_to_all(pieces.astype(jnp.bfloat16), 'expert', split_axis=0, conca...  20 us
    all_to_all x1, waiting for transfers between devices, copy_for_each(): return lax.all_to_all(copies, axis, split_axis=0, concat_axis=0, tiled=True)  15.2 us
    all_to_all x1, starting transfers between devices, copy_for_each(): return lax.all_to_all(copies, axis, split_axis=0, concat_axis=0, tiled=True)  3.69 us
    gather x1, local copies, waits for them, and re-layouts, select_rows(): picked = jnp.take_along_axis(blocked, route_index[0, 0][:, :, None], axis=1)  3.68 us
  transfers between devices with their start and end apart: 2, of which 2 were waited for; matrix products, arithmetic and copies ran while one was open for 3% of the time, Pallas kernels for 0%

commit v1 on v0

v1 whole, which is shorter than its diff:
```python
import functools

import jax
import jax.numpy as jnp
from jax import lax
from jax.experimental import pallas as pl
from jax.experimental.pallas import tpu as pltpu
from jax.sharding import PartitionSpec as P

MESH = pl.DeviceIdType.MESH
QBLOCK = 128
NY, NX, NZ, NC = 4, 4, 16, 2
NS = NX * NC
CHUNKS = 4

momentum_decay = 0.9
step_rate = 0.5
epsilon = 1e-06
range_limit = 448.0
BF = jnp.bfloat16
F32 = jnp.float32


def idiv(v, d):
    if d == 3:
        return (v * 171) >> 9
    return idiv(v >> (3 if d == 24 else 4), 3)


def split_jip(r):
    j = idiv(r, 24)
    rem = r - j * 24
    i = idiv(rem, 3)
    return j, i, rem - i * 3


def split_ijp(r):
    i = idiv(r, 48)
    rem = r - i * 48
    j = idiv(rem, 3)
    return i, j, rem - j * 3


def dot(a, b):
    return jnp.dot(a, b, preferred_element_type=F32)


def iota(shape, dim):
    return lax.broadcasted_iota(jnp.int32, shape, dim)


def onehot(cond):
    return jnp.where(cond, 1.0, 0.0).astype(BF)


def kernel(
    C,
    grad, mom, mas, cur, nxt, live, route, act,
    nm_out, out,
    gs, mom_v, mas_v, act_v,
    rl, rr, sa1, sa2, pleft, pright,
    zs1, zr1, ss1, sr1, ss2, sr2, zs2, zr2, wl, wr, wo,
    selp, p1, p2, p3, m1, m2,
    lsem, asend, arecv, zsend, zrecv, ssend, srecv, dsend, drecv,
):
    n = CHUNKS
    e = lax.axis_index("expert")
    y = lax.axis_index("dp")
    x, z, c = e // (NZ * NC), (e // NC) % NZ, e % NC
    rows = grad.shape[0]
    half = rows // 2

    def at(dy=0, dx=0, dz=0, dc=0):
        ex = (lax.rem(x + dx, NX) * NZ + lax.rem(z + dz, NZ)) * NC + lax.rem(c + dc, NC)
        return (lax.rem(y + dy, NY), ex)

    def at_i(i):
        return at(dx=i // NC, dc=i % NC)

    def remote(src, dst, ssem, rsem, device):
        return pltpu.make_async_remote_copy(
            src_ref=src, dst_ref=dst, send_sem=ssem, recv_sem=rsem,
            device_id=device, device_id_type=MESH,
        )

    barrier = pltpu.get_barrier_semaphore()
    peers = [at(dz=j) for j in range(1, NZ)]
    peers += [at_i(i) for i in range(1, NS)]
    peers += [at(dy=1), at(dy=3)]
    for device in peers:
        pl.semaphore_signal(barrier, inc=1, device_id=device, device_id_type=MESH)

    locals_ = {}
    k_width = C * n
    for k in range(n):
        for b in (2, 1, 3, 0):
            off = pl.multiple_of(lax.rem(y + b, NY) * k_width + k * C, 128)
            cp = pltpu.make_async_copy(grad.at[:, pl.ds(off, C)], gs.at[b, k], lsem.at[b * n + k])
            cp.start()
            locals_[b, k] = cp
    cp_act = pltpu.make_async_copy(act, act_v, lsem.at[4 * n])
    cp_mom = pltpu.make_async_copy(mom, mom_v, lsem.at[4 * n + 1])
    cp_mas = pltpu.make_async_copy(mas, mas_v, lsem.at[4 * n + 2])
    cp_act.start()
    cp_mom.start()
    cp_mas.start()

    r_col = iota((rows, 1), 0)
    r_row = iota((1, rows), 1)
    lanes = iota((rows, rows), 1)
    subl = iota((rows, rows), 0)
    j, i, p = split_jip(r_col)
    dx, dc = i >> 1, i & 1
    dest = ((x + dx) & 3) * 96 + ((z + j) & 15) * 6 + ((c + dc) & 1) * 3 + p
    p1[...] = onehot(lanes == dest)
    p3[...] = onehot(lanes == i * 48 + j * 3 + p)
    i, j, p = split_ijp(r_col)
    p2[...] = onehot(lanes == j * 24 + i * 3 + p)
    dx, dc = i >> 1, i & 1
    nslot = (((x + dx) & 3) * NZ + ((z + j) & 15)) * NC + ((c + dc) & 1)
    pick = onehot(iota((rows, 128), 1) == nslot)
    experts = mom_v.shape[1]
    three = 3 * experts
    nvals = jnp.broadcast_to(nxt[...].astype(F32), (128, three)).astype(BF)
    expert_of = dot(pick, nvals).astype(jnp.int32)
    m2[...] = onehot(expert_of + experts * p == iota((rows, three), 1))

    i, j, p = split_ijp(r_row)
    dx, dc = i >> 1, i & 1
    cslot = (((x - dx) & 3) * NZ + ((z - j) & 15)) * NC + ((c + dc) & 1)
    pick = onehot(iota((128, rows), 0) == cslot)
    cvals = jnp.broadcast_to(cur[...].astype(F32), (128, 128)).T.astype(BF)
    expert_of = dot(cvals, pick).astype(jnp.int32)[0:1, :]
    m1[...] = onehot(expert_of + experts * p == iota((three, rows), 0))

    j, i, p = split_jip(r_row)
    dx, dc = i >> 1, i & 1
    source = ((x - dx) & 3) * 96 + ((z - j) & 15) * 6 + ((c + dc) & 1) * 3 + p
    p4 = onehot(subl == source)
    cp_act.wait()
    blocks, rb = route.shape
    for q in range(blocks):
        hit = jnp.where(route[q : q + 1, :] == iota((rb, rb), 0), 1.0, 0.0).astype(F32)
        picked = dot(hit.T.astype(BF), act_v[q * rb : (q + 1) * rb, :])
        alive = iota((rb, 1), 0) + q * rb < live[...]
        picked = jnp.where(alive, picked, 0.0).astype(BF)
        selp[q * rb : (q + 1) * rb, :] = dot(picked, p4).astype(BF)

    pl.semaphore_wait(barrier, len(peers))

    ends = []

    def a1(k):
        for b in (2, 1, 3):
            locals_[b, k].wait()
        up, down = at(dy=1), at(dy=3)
        lo, hi = pl.ds(0, half), pl.ds(half, half)
        for args in (
            (gs.at[2, k, lo], rl.at[k], asend.at[0, k], arecv.at[0, k], up),
            (gs.at[2, k, hi], rr.at[k], asend.at[1, k], arecv.at[1, k], down),
            (gs.at[1, k, hi], pleft.at[k, hi], asend.at[2, k], arecv.at[2, k], up),
            (gs.at[3, k, lo], pright.at[k, lo], asend.at[3, k], arecv.at[3, k], down),
        ):
            cp = remote(*args)
            cp.start()
            ends.append(cp)

    def a2(k):
        up, down = at(dy=1), at(dy=3)
        lo, hi = pl.ds(0, half), pl.ds(half, half)
        remote(rl.at[k], rl.at[k], asend.at[0, k], arecv.at[0, k], up).wait_recv()
        sa1[k] = (gs[1, k, 0:half].astype(F32) + rl[k].astype(F32)).astype(BF)
        cp = remote(sa1.at[k], pleft.at[k, lo], asend.at[4, k], arecv.at[2, k], up)
        cp.start()
        ends.append(cp)
        remote(rr.at[k], rr.at[k], asend.at[1, k], arecv.at[1, k], down).wait_recv()
        sa2[k] = (gs[3, k, half:].astype(F32) + rr[k].astype(F32)).astype(BF)
        cp = remote(sa2.at[k], pright.at[k, hi], asend.at[5, k], arecv.at[3, k], down)
        cp.start()
        ends.append(cp)

    def exchange_z(k, send, recv, s):
        for j in range(1, NZ):
            remote(send.at[k, j], recv.at[k, j], zsend.at[s, k], zrecv.at[s, k], at(dz=j)).start()
        every = pl.ds(1, NZ - 1)
        ends.append(remote(send.at[k, every], recv.at[k, every], zsend.at[s, k], zrecv.at[s, k], at(dz=1)))

    def arrived_z(k, recv, s):
        every = pl.ds(1, NZ - 1)
        remote(recv.at[k, every], recv.at[k, every], zsend.at[s, k], zrecv.at[s, k], at(dz=1)).wait_recv()

    def exchange_s(k, send, recv, s):
        for i in range(NS - 1, 0, -1):
            remote(send.at[k, i], recv.at[k, i], ssend.at[s, k], srecv.at[s, k], at_i(i)).start()
        every = pl.ds(1, NS - 1)
        ends.append(remote(send.at[k, every], recv.at[k, every], ssend.at[s, k], srecv.at[s, k], at_i(1)))

    def arrived_s(k, recv, s):
        every = pl.ds(1, NS - 1)
        remote(recv.at[k, every], recv.at[k, every], ssend.at[s, k], srecv.at[s, k], at_i(1)).wait_recv()

    def a3(k):
        remote(pleft.at[k], pleft.at[k], asend.at[2, k], arecv.at[2, k], at(dy=1)).wait_recv()
        remote(pright.at[k], pright.at[k], asend.at[3, k], arecv.at[3, k], at(dy=3)).wait_recv()
        locals_[0, k].wait()
        total = gs[0, k].astype(F32) + pleft[k].astype(F32) + pright[k].astype(F32)
        moved = dot(p1[...], total.astype(BF)).reshape(NZ, 24, C).astype(BF)
        zs1[k] = moved
        zr1[k, 0] = moved[0]
        exchange_z(k, zs1, zr1, 0)

    def b1(k):
        arrived_z(k, zr1, 0)
        held = zr1[k].astype(F32).reshape(rows, C).astype(BF)
        moved = dot(p2[...], held).reshape(NS, 48, C).astype(BF)
        ss1[k] = moved
        sr1[k, 0] = moved[0]
        exchange_s(k, ss1, sr1, 0)

    def b2(k):
        arrived_s(k, sr1, 0)
        totals = dot(m1[...], sr1[k].reshape(rows, C))
        cols = slice(k * C, (k + 1) * C)
        new_momentum = momentum_decay * mom_v[:, :, cols].reshape(three, C) + totals
        nm_out[:, :, cols] = new_momentum.reshape(3, experts, C)
        master = mas_v[:, :, cols].reshape(three, C)
        weights = master - step_rate * new_momentum
        parts = []
        for b in range(C // QBLOCK):
            lanes_b = slice(b * QBLOCK, (b + 1) * QBLOCK)
            top = jnp.max(jnp.abs(master[:, lanes_b]), axis=1, keepdims=True)
            scale = (top / range_limit + epsilon).astype(BF).astype(F32)
            quantized = jnp.clip(weights[:, lanes_b] / scale, -range_limit, range_limit).astype(BF)
            parts.append((quantized.astype(F32) * scale).astype(BF))
        restored = parts[0] if len(parts) == 1 else jnp.concatenate(parts, axis=1)
        moved = dot(m2[...], restored).reshape(NS, 48, C).astype(BF)
        ss2[k] = moved
        sr2[k, 0] = moved[0]
        exchange_s(k, ss2, sr2, 1)

    def c1(k):
        arrived_s(k, sr2, 1)
        moved = dot(p3[...], sr2[k].reshape(rows, C)).reshape(NZ, 24, C).astype(BF)
        zs2[k] = moved
        zr2[k, 0] = moved[0]
        exchange_z(k, zs2, zr2, 1)

    lo8, hi8 = pl.ds(0, NZ // 2), pl.ds(NZ // 2, NZ // 2)

    def d1(k):
        arrived_z(k, zr2, 1)
        up, down = at(dy=1), at(dy=3)
        for args in (
            (zr2.at[k, lo8], wl.at[k, lo8], dsend.at[0, k], drecv.at[0, k], up),
            (zr2.at[k, hi8], wr.at[k, hi8], dsend.at[1, k], drecv.at[1, k], down),
            (zr2.at[k, hi8], wl.at[k, hi8], dsend.at[2, k], drecv.at[2, k], up),
            (zr2.at[k, lo8], wr.at[k, lo8], dsend.at[3, k], drecv.at[3, k], down),
        ):
            cp = remote(*args)
            cp.start()
            ends.append(cp)

    def multiply(k, held, b):
        weight = held[k].astype(F32).reshape(rows, C).astype(BF)
        product = dot(selp[...], weight).astype(BF)
        off = pl.multiple_of(lax.rem(y + b, NY) * k_width + k * C, 128)
        out[:, pl.ds(off, C)] = product

    def d2(k):
        up, down = at(dy=1), at(dy=3)
        remote(wl.at[k, lo8], wl.at[k, lo8], dsend.at[0, k], drecv.at[0, k], up).wait_recv()
        cp = remote(wl.at[k, lo8], wo.at[k, lo8], dsend.at[4, k], drecv.at[4, k], up)
        cp.start()
        ends.append(cp)
        remote(wr.at[k, hi8], wr.at[k, hi8], dsend.at[1, k], drecv.at[1, k], down).wait_recv()
        cp = remote(wr.at[k, hi8], wo.at[k, hi8], dsend.at[5, k], drecv.at[5, k], down)
        cp.start()
        ends.append(cp)
        multiply(k, zr2, 0)

    def d3(k):
        up, down = at(dy=1), at(dy=3)
        remote(wl.at[k, hi8], wl.at[k, hi8], dsend.at[2, k], drecv.at[2, k], up).wait_recv()
        multiply(k, wl, 3)
        remote(wr.at[k, lo8], wr.at[k, lo8], dsend.at[3, k], drecv.at[3, k], down).wait_recv()
        multiply(k, wr, 1)
        remote(wo.at[k, lo8], wo.at[k, lo8], dsend.at[4, k], drecv.at[4, k], up).wait_recv()
        remote(wo.at[k, hi8], wo.at[k, hi8], dsend.at[5, k], drecv.at[5, k], down).wait_recv()
        multiply(k, wo, 2)

    a1(0); a1(1); a2(0); a3(0); a1(2)
    cp_mom.wait()
    cp_mas.wait()
    a2(1); a3(1); a1(3); a2(2); a3(2); b1(0)
    a2(3); a3(3); b2(0); b1(1); c1(0); b2(1); b1(2); c1(1); b2(2); b1(3); c1(2); b2(3)
    d1(0); c1(3); d2(0); d1(1); d3(0); d2(1); d1(2); d3(1); d2(2); d1(3); d3(2); d2(3); d3(3)
    for cp in ends:
        cp.wait_send()


def shards(grads, momentum, master, current_slots, next_slots, live_counts, route_index, activations):
    grad = grads[0, 0]
    rows, width = grad.shape
    columns = momentum.shape[2]
    experts = momentum.shape[1]
    n = CHUNKS
    C = columns // n
    out_rows, hidden = activations.shape[2:]
    half = rows // 2
    any_ = pl.BlockSpec(memory_space=pl.ANY)
    vmem = pl.BlockSpec(memory_space=pltpu.VMEM)

    def buf(*shape):
        return pltpu.VMEM(shape, BF)

    zbuf = buf(n, NZ, 24, C)
    sbuf = buf(n, NS, 48, C)
    sems = pltpu.SemaphoreType.DMA
    new_momentum, expert_out = pl.pallas_call(
        functools.partial(kernel, C),
        out_shape=(
            jax.ShapeDtypeStruct(momentum.shape, F32),
            jax.ShapeDtypeStruct((out_rows, width), BF),
        ),
        in_specs=[any_, any_, any_, vmem, vmem, vmem, vmem, any_],
        out_specs=(vmem, vmem),
        scratch_shapes=[
            buf(NY, n, rows, C),
            pltpu.VMEM(momentum.shape, F32),
            pltpu.VMEM(momentum.shape, F32),
            buf(out_rows, hidden),
            buf(n, half, C), buf(n, half, C), buf(n, half, C), buf(n, half, C),
            buf(n, rows, C), buf(n, rows, C),
            zbuf, zbuf, sbuf, sbuf, sbuf, sbuf, zbuf, zbuf, zbuf, zbuf, zbuf,
            buf(out_rows, hidden),
            buf(rows, rows), buf(rows, rows), buf(rows, rows),
            buf(3 * experts, rows), buf(rows, 3 * experts),
            sems((4 * n + 3,)),
            sems((6, n)), sems((4, n)),
            sems((2, n)), sems((2, n)),
            sems((2, n)), sems((2, n)),
            sems((6, n)), sems((6, n)),
        ],
        compiler_params=pltpu.CompilerParams(
            collective_id=0, has_side_effects=True, vmem_limit_bytes=40 * 1024 * 1024
        ),
        name="step",
    )(
        grad, momentum, master, current_slots, next_slots, live_counts,
        route_index[0, 0], activations[0, 0],
    )
    return new_momentum, expert_out[None, None]


def solution(mesh):
    in_specs = (
        P("dp", "expert", None, None),
        P("expert", None, "dp"),
        P("expert", None, "dp"),
        P(),
        P(),
        P("dp", "expert"),
        P("dp", "expert", None, None),
        P("dp", "expert", None, None),
    )
    out_specs = (P("expert", None, "dp"), P("dp", "expert", None, None))
    return jax.shard_map(shards, mesh=mesh, in_specs=in_specs, out_specs=out_specs, check_vma=False)
```

time: 160 us -> 87.9 us (0.55); the launches traced: 158 us -> 87.6 us
  Pallas kernels: 0 us -> 77.7 us
  blocking collectives: 70.6 us -> 0 us
  waiting for transfers between devices: 45.8 us -> 0 us
  starting transfers between devices: 23.7 us -> 0 us
  matrix products: 3.26 us -> 0 us
  local copies, waits for them, and re-layouts: 11.6 us -> 8.66 us
    pallas_call x0 -> x1, Pallas kernels: none -> 77.7 us  [shards(): pl.pallas_call(functools.partial(kernel, C), out_shape=(jax.ShapeDtypeStr...]
    all_to_all x2 -> x0, blocking collectives: 70.6 us -> none  [the longest x1 45.6 us: sent_together(): lax.all_to_all(both, axis, split_axis=split_dim, concat_axis=concat_dim,...]
    all_to_all x2 -> x0, waiting for transfers between devices: 45.8 us -> none  [the longest x1 30.6 us: shards(): lax.all_to_all(pieces.astype(jnp.bfloat16), 'expert', split_axis=0, conca...]
    all_to_all x2 -> x0, starting transfers between devices: 23.7 us -> none  [the longest x1 20 us: shards(): lax.all_to_all(pieces.astype(jnp.bfloat16), 'expert', split_axis=0, conca...]
    unnamed x16 -> x14, local copies, waits for them, and re-layouts: 2.06 us -> 8.66 us
    gather x1 -> x0, local copies, waits for them, and re-layouts: 3.68 us -> none  [select_rows(): picked = jnp.take_along_axis(blocked, route_index[0, 0][:, :, None], axis=1)]
    dot_general x4 -> x0, matrix products: 3.26 us -> none  [the longest x1 2.6 us: shards(): jnp.dot(selected, gathered_copies(weight_cols, 'dp', 1), preferred_elemen...]
    convert_element_type x7 -> x0, local copies, waits for them, and re-layouts: 2.21 us -> none  [the longest x1 1.01 us: shards(): pieces.astype(jnp.bfloat16)]
  transfers between devices with their start and end apart: 2 -> 0, of which waited for: 2 -> 0; matrix products, arithmetic and copies ran while one was open for 3% -> 0% of each run, Pallas kernels for 0% -> 0%
where the time goes in v1:
time: 87.9 us; the launch traced here: 87.6 us
  Pallas kernels  77.7 us (88%)
  local copies, waits for them, and re-layouts  8.66 us (10%)
  between operations  1.3 us (1%)
    pallas_call x1, Pallas kernels, shards(): pl.pallas_call(functools.partial(kernel, C), out_shape=(jax.ShapeDtypeStr...  77.7 us
    unnamed x14, local copies, waits for them, and re-layouts  8.66 us

profile of v1, /device:TPU:6, one launch (start us, length us, event | category | flops | bytes accessed | tf_op | source)
XLA Modules:
  0.0 87.6 jit_solution(13969235854271525544)
XLA Ops:
  1.3 0.8 copy.10.cur
  2.0 0.8 copy.11.nxt
  2.8 0.0 copy-start
  2.8 1.4 %copy-done = bf16[1,1,384,2048]{3,2,1,0:T(8,128)(2,1)S(1)} copy-done((bf16[1,1,384,2048]{3,2,1,0:T(8,128)(2,1)S(1)}, bf16[1,1,384,2048]{3,2,1,0:T(8,128)(2,1)}, u32[]{:S(2)}) %copy-start) | copy-done | bytes 1572888
  4.2 0.0 copy-start.1
  4.2 1.0 %copy-done.1 = f32[3,64,512]{2,1,0:T(8,128)S(1)} copy-done((f32[3,64,512]{2,1,0:T(8,128)S(1)}, f32[3,64,512]{2,1,0:T(8,128)}, u32[]{:S(2)}) %copy-start.1) | copy-done | bytes 393240
  5.2 0.0 copy-start.2
  5.2 1.0 %copy-done.2 = f32[3,64,512]{2,1,0:T(8,128)S(1)} copy-done((f32[3,64,512]{2,1,0:T(8,128)S(1)}, f32[3,64,512]{2,1,0:T(8,128)}, u32[]{:S(2)}) %copy-start.2) | copy-done | bytes 393240
  6.2 0.0 copy-start.3
  6.2 1.0 %copy-done.3 = bf16[1,1,512,384]{3,2,1,0:T(8,128)(2,1)S(1)} copy-done((bf16[1,1,512,384]{3,2,1,0:T(8,128)(2,1)S(1)}, bf16[1,1,512,384]{3,2,1,0:T(8,128)(2,1)}, u32[]{:S(2)}) %copy-start.3) | copy-done | bytes 393240
  7.2 0.0 copy-start.4
  7.2 0.7 copy-done.4
  7.9 77.7 %step.1 = (f32[3,64,512]{2,1,0:T(8,128)S(1)}, bf16[512,2048]{1,0:T(8,128)(2,1)S(1)}) custom-call(bf16[384,2048]{1,0:T(8,128)(2,1)S(1)} %bitcast.5, f32[3,64,512]{2,1,0:T(8,128)S(1)} %copy-done.1, f32[3,64,512]{2,1,0:T(8,128)S(1)} %copy-done.2, s32[128,1]{1,0:T(8,128)S(1)} %copy.10.cur, s32[128,1]{1,0:T(8,128)S(1)} %copy.11.nxt, s32[1,1]{1,0:T(1,128)S(6)} %copy.14.live, ...), custom_call_target="tpu_custom_call" | custom-call | tf_op jit(solution)/shard_map/step/pallas_call | solution.py:319
  85.6 0.7 copy.15
  86.3 1.3 %copy.16 = bf16[1,1,512,2048]{3,2,1,0:T(8,128)(2,1)} copy(bf16[1,1,512,2048]{3,2,1,0:T(8,128)(2,1)S(1)} %bitcast.4) | data formatting | bytes 4194304
Async XLA Ops:
  2.8 1.4 %copy-start = (bf16[1,1,384,2048]{3,2,1,0:T(8,128)(2,1)S(1)}, bf16[1,1,384,2048]{3,2,1,0:T(8,128)(2,1)}, u32[]{:S(2)}) copy-start(bf16[1,1,384,2048]{3,2,1,0:T(8,128)(2,1)} %param.8) | copy-start | bytes 4718596
  4.2 1.0 %copy-start.1 = (f32[3,64,512]{2,1,0:T(8,128)S(1)}, f32[3,64,512]{2,1,0:T(8,128)}, u32[]{:S(2)}) copy-start(f32[3,64,512]{2,1,0:T(8,128)} %mom.1) | copy-start | bytes 1179652
  5.2 1.0 %copy-start.2 = (f32[3,64,512]{2,1,0:T(8,128)S(1)}, f32[3,64,512]{2,1,0:T(8,128)}, u32[]{:S(2)}) copy-start(f32[3,64,512]{2,1,0:T(8,128)} %mas.1) | copy-start | bytes 1179652
  6.2 1.0 %copy-start.3 = (bf16[1,1,512,384]{3,2,1,0:T(8,128)(2,1)S(1)}, bf16[1,1,512,384]{3,2,1,0:T(8,128)(2,1)}, u32[]{:S(2)}) copy-start(bf16[1,1,512,384]{3,2,1,0:T(8,128)(2,1)} %param.15) | copy-start | bytes 1179652
  7.2 0.7 copy-start.4

commit v2 on v1

--- a/solution.py
+++ b/solution.py
@@ -55,13 +55,13 @@
 
 def kernel(
     C,
-    grad, mom, mas, cur, nxt, live, route, act,
+    grad, mom, mas, cur_h, nxt_h, live, route_h, act,
     nm_out, out,
-    gs, mom_v, mas_v, act_v,
+    gs, mom_v, mas_v, act_v, cur, nxt, route,
     rl, rr, sa1, sa2, pleft, pright,
     zs1, zr1, ss1, sr1, ss2, sr2, zs2, zr2, wl, wr, wo,
-    selp, p1, p2, p3, m1, m2,
-    lsem, asend, arecv, zsend, zrecv, ssend, srecv, dsend, drecv,
+    selp, p1, p2, p3, p4, m1, m2,
+    lsem, asend, arecv, zsend, zrecv, ssend, srecv, dsend, drecv, tsem,
 ):
     n = CHUNKS
     e = lax.axis_index("expert")
@@ -84,75 +84,92 @@
         )
 
     barrier = pltpu.get_barrier_semaphore()
-    peers = [at(dz=j) for j in range(1, NZ)]
+    peers = [at(dz=1), at(dz=NZ - 1)]
     peers += [at_i(i) for i in range(1, NS)]
     peers += [at(dy=1), at(dy=3)]
     for device in peers:
         pl.semaphore_signal(barrier, inc=1, device_id=device, device_id_type=MESH)
 
-    locals_ = {}
+    staged = {}
     k_width = C * n
     for k in range(n):
         for b in (2, 1, 3, 0):
             off = pl.multiple_of(lax.rem(y + b, NY) * k_width + k * C, 128)
-            cp = pltpu.make_async_copy(grad.at[:, pl.ds(off, C)], gs.at[b, k], lsem.at[b * n + k])
-            cp.start()
-            locals_[b, k] = cp
-    cp_act = pltpu.make_async_copy(act, act_v, lsem.at[4 * n])
-    cp_mom = pltpu.make_async_copy(mom, mom_v, lsem.at[4 * n + 1])
-    cp_mas = pltpu.make_async_copy(mas, mas_v, lsem.at[4 * n + 2])
-    cp_act.start()
-    cp_mom.start()
-    cp_mas.start()
-
-    r_col = iota((rows, 1), 0)
-    r_row = iota((1, rows), 1)
-    lanes = iota((rows, rows), 1)
-    subl = iota((rows, rows), 0)
-    j, i, p = split_jip(r_col)
-    dx, dc = i >> 1, i & 1
-    dest = ((x + dx) & 3) * 96 + ((z + j) & 15) * 6 + ((c + dc) & 1) * 3 + p
-    p1[...] = onehot(lanes == dest)
-    p3[...] = onehot(lanes == i * 48 + j * 3 + p)
-    i, j, p = split_ijp(r_col)
-    p2[...] = onehot(lanes == j * 24 + i * 3 + p)
-    dx, dc = i >> 1, i & 1
-    nslot = (((x + dx) & 3) * NZ + ((z + j) & 15)) * NC + ((c + dc) & 1)
-    pick = onehot(iota((rows, 128), 1) == nslot)
+            staged[b, k] = pltpu.make_async_copy(grad.at[:, pl.ds(off, C)], gs.at[b, k], lsem.at[b * n + k])
+    small = [(act, act_v), (route_h, route), (cur_h, cur), (nxt_h, nxt), (mom, mom_v), (mas, mas_v)]
+    small = [pltpu.make_async_copy(src, dst, lsem.at[4 * n + at_]) for at_, (src, dst) in enumerate(small)]
+    cp_act, cp_route, cp_cur, cp_nxt, cp_mom, cp_mas = small
+    for k in range(n):
+        for b in (2, 1, 3, 0):
+            staged[b, k].start()
+    for cp in (cp_cur, cp_nxt, cp_route, cp_act, cp_mom, cp_mas):
+        cp.start()
+
     experts = mom_v.shape[1]
     three = 3 * experts
-    nvals = jnp.broadcast_to(nxt[...].astype(F32), (128, three)).astype(BF)
-    expert_of = dot(pick, nvals).astype(jnp.int32)
-    m2[...] = onehot(expert_of + experts * p == iota((rows, three), 1))
-
-    i, j, p = split_ijp(r_row)
-    dx, dc = i >> 1, i & 1
-    cslot = (((x - dx) & 3) * NZ + ((z - j) & 15)) * NC + ((c + dc) & 1)
-    pick = onehot(iota((128, rows), 0) == cslot)
-    cvals = jnp.broadcast_to(cur[...].astype(F32), (128, 128)).T.astype(BF)
-    expert_of = dot(cvals, pick).astype(jnp.int32)[0:1, :]
-    m1[...] = onehot(expert_of + experts * p == iota((three, rows), 0))
-
-    j, i, p = split_jip(r_row)
-    dx, dc = i >> 1, i & 1
-    source = ((x - dx) & 3) * 96 + ((z - j) & 15) * 6 + ((c + dc) & 1) * 3 + p
-    p4 = onehot(subl == source)
-    cp_act.wait()
-    blocks, rb = route.shape
-    for q in range(blocks):
+
+    def build_p1():
+        j, i, p = split_jip(iota((rows, 1), 0))
+        dest = ((x + (i >> 1)) & 3) * 96 + ((z + j) & 15) * 6 + ((c + (i & 1)) & 1) * 3 + p
+        p1[...] = onehot(iota((rows, rows), 1) == dest)
+
+    def build_p2():
+        i, j, p = split_ijp(iota((rows, 1), 0))
+        p2[...] = onehot(iota((rows, rows), 1) == j * 24 + i * 3 + p)
+
+    def build_p3():
+        j, i, p = split_jip(iota((rows, 1), 0))
+        p3[...] = onehot(iota((rows, rows), 1) == i * 48 + j * 3 + p)
+
+    def build_m1():
+        i, j, p = split_ijp(iota((1, rows), 1))
+        slot = (((x - (i >> 1)) & 3) * NZ + ((z - j) & 15)) * NC + ((c + (i & 1)) & 1)
+        pick = onehot(iota((128, rows), 0) == slot)
+        cp_cur.wait()
+        values = jnp.broadcast_to(cur[...].astype(F32), (16, 128)).astype(BF)
+        expert_of = dot(values, pick).astype(jnp.int32)[0:1, :]
+        m1[...] = onehot(expert_of + experts * p == iota((three, rows), 0))
+
+    def build_m2():
+        i, j, p = split_ijp(iota((rows, 1), 0))
+        slot = (((x + (i >> 1)) & 3) * NZ + ((z + j) & 15)) * NC + ((c + (i & 1)) & 1)
+        pick = onehot(iota((rows, 128), 1) == slot)
+        cp_nxt.wait()
+        values = jnp.broadcast_to(nxt[...].astype(F32), (128, 128)).T.astype(BF)
+        values = jnp.concatenate([values, values], axis=1)[:, 0:three]
+        expert_of = dot(pick, values).astype(jnp.int32)
+        m2[...] = onehot(expert_of + experts * p == iota((rows, three), 1))
+
+    def build_p4():
+        j, i, p = split_jip(iota((1, rows), 1))
+        source = ((x - (i >> 1)) & 3) * 96 + ((z - j) & 15) * 6 + ((c + (i & 1)) & 1) * 3 + p
+        p4[...] = onehot(iota((rows, rows), 0) == source)
+        cp_act.wait()
+        cp_route.wait()
+
+    def select(q):
+        rb = route.shape[1]
         hit = jnp.where(route[q : q + 1, :] == iota((rb, rb), 0), 1.0, 0.0).astype(F32)
         picked = dot(hit.T.astype(BF), act_v[q * rb : (q + 1) * rb, :])
         alive = iota((rb, 1), 0) + q * rb < live[...]
         picked = jnp.where(alive, picked, 0.0).astype(BF)
-        selp[q * rb : (q + 1) * rb, :] = dot(picked, p4).astype(BF)
+        selp[q * rb : (q + 1) * rb, :] = dot(picked, p4[...]).astype(BF)
 
     pl.semaphore_wait(barrier, len(peers))
 
     ends = []
+
+    def tell(r):
+        for way, dz in ((0, 1 << r), (1, NZ - (1 << r))):
+            pl.semaphore_signal(tsem.at[r, way], inc=1, device_id=at(dz=dz), device_id_type=MESH)
+
+    def hear(r):
+        pl.semaphore_wait(tsem.at[r, 0], 1)
+        pl.semaphore_wait(tsem.at[r, 1], 1)
 
     def a1(k):
         for b in (2, 1, 3):
-            locals_[b, k].wait()
+            staged[b, k].wait()
         up, down = at(dy=1), at(dy=3)
         lo, hi = pl.ds(0, half), pl.ds(half, half)
         for args in (
@@ -202,7 +219,7 @@
     def a3(k):
         remote(pleft.at[k], pleft.at[k], asend.at[2, k], arecv.at[2, k], at(dy=1)).wait_recv()
         remote(pright.at[k], pright.at[k], asend.at[3, k], arecv.at[3, k], at(dy=3)).wait_recv()
-        locals_[0, k].wait()
+        staged[0, k].wait()
         total = gs[0, k].astype(F32) + pleft[k].astype(F32) + pright[k].astype(F32)
         moved = dot(p1[...], total.astype(BF)).reshape(NZ, 24, C).astype(BF)
         zs1[k] = moved
@@ -288,12 +305,12 @@
         remote(wo.at[k, hi8], wo.at[k, hi8], dsend.at[5, k], drecv.at[5, k], down).wait_recv()
         multiply(k, wo, 2)
 
-    a1(0); a1(1); a2(0); a3(0); a1(2)
+    a1(0); tell(0); a1(1); build_p1(); hear(0); tell(1); a2(0); hear(1); tell(2); a1(2); build_p2(); hear(2); a3(0)
+    a2(1); build_m1(); build_m2(); a3(1); a1(3); a2(2); build_p3(); build_p4(); a3(2)
     cp_mom.wait()
     cp_mas.wait()
-    a2(1); a3(1); a1(3); a2(2); a3(2); b1(0)
-    a2(3); a3(3); b2(0); b1(1); c1(0); b2(1); b1(2); c1(1); b2(2); b1(3); c1(2); b2(3)
-    d1(0); c1(3); d2(0); d1(1); d3(0); d2(1); d1(2); d3(1); d2(2); d1(3); d3(2); d2(3); d3(3)
+    b1(0); select(0); a2(3); a3(3); b2(0); b1(1); select(1); c1(0); b2(1); b1(2); c1(1); b2(2); b1(3)
+    c1(2); b2(3); select(2); select(3); d1(0); c1(3); d2(0); d1(1); d3(0); d2(1); d1(2); d3(1); d2(2); d1(3); d3(2); d2(3); d3(3)
     for cp in ends:
         cp.wait_send()
 
@@ -307,7 +324,7 @@
     C = columns // n
     out_rows, hidden = activations.shape[2:]
     half = rows // 2
-    any_ = pl.BlockSpec(memory_space=pl.ANY)
+    hbm = pl.BlockSpec(memory_space=pltpu.MemorySpace.HBM)
     vmem = pl.BlockSpec(memory_space=pltpu.VMEM)
 
     def buf(*shape):
@@ -316,38 +333,43 @@
     zbuf = buf(n, NZ, 24, C)
     sbuf = buf(n, NS, 48, C)
     sems = pltpu.SemaphoreType.DMA
+    held = lambda a: pltpu.with_memory_space_constraint(a, pltpu.MemorySpace.HBM)
     new_momentum, expert_out = pl.pallas_call(
         functools.partial(kernel, C),
         out_shape=(
             jax.ShapeDtypeStruct(momentum.shape, F32),
             jax.ShapeDtypeStruct((out_rows, width), BF),
         ),
-        in_specs=[any_, any_, any_, vmem, vmem, vmem, vmem, any_],
+        in_specs=[hbm, hbm, hbm, hbm, hbm, vmem, hbm, hbm],
         out_specs=(vmem, vmem),
         scratch_shapes=[
             buf(NY, n, rows, C),
             pltpu.VMEM(momentum.shape, F32),
             pltpu.VMEM(momentum.shape, F32),
             buf(out_rows, hidden),
+            pltpu.VMEM((1, current_slots.shape[0]), jnp.int32),
+            pltpu.VMEM((1, current_slots.shape[0]), jnp.int32),
+            pltpu.VMEM(route_index.shape[2:], jnp.int32),
             buf(n, half, C), buf(n, half, C), buf(n, half, C), buf(n, half, C),
             buf(n, rows, C), buf(n, rows, C),
             zbuf, zbuf, sbuf, sbuf, sbuf, sbuf, zbuf, zbuf, zbuf, zbuf, zbuf,
             buf(out_rows, hidden),
-            buf(rows, rows), buf(rows, rows), buf(rows, rows),
+            buf(rows, rows), buf(rows, rows), buf(rows, rows), buf(rows, rows),
             buf(3 * experts, rows), buf(rows, 3 * experts),
-            sems((4 * n + 3,)),
+            sems((4 * n + 6,)),
             sems((6, n)), sems((4, n)),
             sems((2, n)), sems((2, n)),
             sems((2, n)), sems((2, n)),
             sems((6, n)), sems((6, n)),
+            pltpu.SemaphoreType.REGULAR((3, 2)),
         ],
         compiler_params=pltpu.CompilerParams(
             collective_id=0, has_side_effects=True, vmem_limit_bytes=40 * 1024 * 1024
         ),
         name="step",
     )(
-        grad, momentum, master, current_slots, next_slots, live_counts,
-        route_index[0, 0], activations[0, 0],
+        held(grad), held(momentum), held(master), held(current_slots.reshape(1, -1)), held(next_slots.reshape(1, -1)), live_counts,
+        held(route_index[0, 0]), held(activations[0, 0]),
     )
     return new_momentum, expert_out[None, None]
 

time: 87.9 us -> 76.6 us (0.87)
  local copies, waits for them, and re-layouts: 8.66 us -> 2.07 us
  Pallas kernels: 77.7 us -> 72.4 us
    unnamed x14 -> x2, local copies, waits for them, and re-layouts: 8.66 us -> 2.07 us
    pallas_call x1, Pallas kernels: 77.7 us -> 72.4 us  [shards(): pl.pallas_call(functools.partial(kernel, C), out_shape=(jax.ShapeDtypeStr...]
where the time goes in v2:
time: 76.6 us; the launch traced here: 75.8 us
  Pallas kernels  72.4 us (95%)
  local copies, waits for them, and re-layouts  2.07 us (3%)
  between operations  1.29 us (2%)
    pallas_call x1, Pallas kernels, shards(): pl.pallas_call(functools.partial(kernel, C), out_shape=(jax.ShapeDtypeStr...  72.4 us
    unnamed x2, local copies, waits for them, and re-layouts  2.07 us

profile of v2, /device:TPU:6, one launch (start us, length us, event | category | flops | bytes accessed | tf_op | source)
XLA Modules:
  0.0 75.8 jit_solution(12346547483360229680)
XLA Ops:
  1.3 72.4 %step.1 = (f32[3,64,512]{2,1,0:T(8,128)S(1)}, bf16[512,2048]{1,0:T(8,128)(2,1)S(1)}) custom-call(bf16[384,2048]{1,0:T(8,128)(2,1)} %bitcast.7, f32[3,64,512]{2,1,0:T(8,128)} %mom.1, f32[3,64,512]{2,1,0:T(8,128)} %mas.1, s32[1,128]{1,0:T(1,128)} %bitcast.10, s32[1,128]{1,0:T(1,128)} %bitcast.11, s32[1,1]{1,0:T(1,128)S(6)} %copy.12.live, s32[4,128]{1,0:T(4,128)} %bitcast.9, ...), custom_call_target="tpu_custom_call" | custom-call | tf_op jit(solution)/shard_map/step/pallas_call | solution.py:337
  73.7 0.7 copy.13
  74.4 1.3 %copy.14 = bf16[1,1,512,2048]{3,2,1,0:T(8,128)(2,1)} copy(bf16[1,1,512,2048]{3,2,1,0:T(8,128)(2,1)S(1)} %bitcast.6) | data formatting | bytes 4194304

commit v3 on v2

v3 whole, which is shorter than its diff:
```python
import functools

import jax
import jax.numpy as jnp
from jax import lax
from jax.experimental import pallas as pl
from jax.experimental.pallas import tpu as pltpu
from jax.sharding import PartitionSpec as P

MESH = pl.DeviceIdType.MESH
QBLOCK = 128
NY, NX, NZ, NC = 4, 4, 16, 2
NS = NX * NC
CHUNKS = 4
FAR_FIRST = sorted(range(1, NZ), key=lambda j: -min(j, NZ - j))

momentum_decay = 0.9
step_rate = 0.5
epsilon = 1e-06
range_limit = 448.0
BF = jnp.bfloat16
F32 = jnp.float32


def idiv(v, d):
    if d == 3:
        return (v * 171) >> 9
    return idiv(v >> (3 if d == 24 else 4), 3)


def split_jip(r):
    j = idiv(r, 24)
    rem = r - j * 24
    i = idiv(rem, 3)
    return j, i, rem - i * 3


def split_ijp(r):
    i = idiv(r, 48)
    rem = r - i * 48
    j = idiv(rem, 3)
    return i, j, rem - j * 3


def dot(a, b):
    return jnp.dot(a, b, preferred_element_type=F32)


def iota(shape, dim):
    return lax.broadcasted_iota(jnp.int32, shape, dim)


def onehot(cond):
    return jnp.where(cond, 1.0, 0.0).astype(BF)


def kernel(
    C,
    grad, mom, mas, cur_h, nxt_h, live, route_h, act,
    nm_out, out,
    gs, mom_v, mas_v, act_v, cur, nxt, route,
    rel, sums, parts_in, zsb, zrb, ssb, srb, wb,
    selp, p1, p2, p3, p4, m1, m2,
    lsem, asend, arecv, zsend, zrecv, ssend, srecv, dsend, drecv, tsem,
):
    n = CHUNKS
    e = lax.axis_index("expert")
    y = lax.axis_index("dp")
    x, z, c = e // (NZ * NC), (e // NC) % NZ, e % NC
    rows = grad.shape[0]
    half = rows // 2

    def at(dy=0, dx=0, dz=0, dc=0):
        ex = (lax.rem(x + dx, NX) * NZ + lax.rem(z + dz, NZ)) * NC + lax.rem(c + dc, NC)
        return (lax.rem(y + dy, NY), ex)

    def at_i(i):
        return at(dx=i // NC, dc=i % NC)

    def remote(src, dst, ssem, rsem, device):
        return pltpu.make_async_remote_copy(
            src_ref=src, dst_ref=dst, send_sem=ssem, recv_sem=rsem,
            device_id=device, device_id_type=MESH,
        )

    barrier = pltpu.get_barrier_semaphore()
    peers = [at(dz=1), at(dz=NZ - 1)]
    peers += [at_i(i) for i in range(1, NS)]
    peers += [at(dy=1), at(dy=3)]
    for device in peers:
        pl.semaphore_signal(barrier, inc=1, device_id=device, device_id_type=MESH)

    k_width = C * n
    for k in range(n):
        for b in (2, 1, 3):
            off = pl.multiple_of(lax.rem(y + b, NY) * k_width + k * C, 128)
            pltpu.make_async_copy(grad.at[:, pl.ds(off, C)], gs.at[b, k], lsem.at[k]).start()
    for k in range(n):
        off = pl.multiple_of(y * k_width + k * C, 128)
        pltpu.make_async_copy(grad.at[:, pl.ds(off, C)], gs.at[0, k], lsem.at[n]).start()
    small = [(act, act_v), (route_h, route), (cur_h, cur), (nxt_h, nxt), (mom, mom_v), (mas, mas_v)]
    small = [pltpu.make_async_copy(src, dst, lsem.at[n + 1 + at_]) for at_, (src, dst) in enumerate(small)]
    cp_act, cp_route, cp_cur, cp_nxt, cp_mom, cp_mas = small
    for cp in (cp_cur, cp_nxt, cp_route, cp_act, cp_mom, cp_mas):
        cp.start()

    def all_of(ref, sem):
        return pltpu.make_async_copy(ref, ref, sem)

    experts = mom_v.shape[1]
    three = 3 * experts

    def build_p1():
        j, i, p = split_jip(iota((rows, 1), 0))
        dest = ((x + (i >> 1)) & 3) * 96 + ((z + j) & 15) * 6 + ((c + (i & 1)) & 1) * 3 + p
        p1[...] = onehot(iota((rows, rows), 1) == dest)

    def build_p2():
        i, j, p = split_ijp(iota((rows, 1), 0))
        p2[...] = onehot(iota((rows, rows), 1) == j * 24 + i * 3 + p)

    def build_p3():
        j, i, p = split_jip(iota((rows, 1), 0))
        p3[...] = onehot(iota((rows, rows), 1) == i * 48 + j * 3 + p)

    def build_m1():
        i, j, p = split_ijp(iota((1, rows), 1))
        slot = (((x - (i >> 1)) & 3) * NZ + ((z - j) & 15)) * NC + ((c + (i & 1)) & 1)
        pick = onehot(iota((128, rows), 0) == slot)
        cp_cur.wait()
        values = jnp.broadcast_to(cur[...].astype(F32), (16, 128)).astype(BF)
        expert_of = dot(values, pick).astype(jnp.int32)[0:1, :]
        m1[...] = onehot(expert_of + experts * p == iota((three, rows), 0))

    def build_m2():
        i, j, p = split_ijp(iota((rows, 1), 0))
        slot = (((x + (i >> 1)) & 3) * NZ + ((z + j) & 15)) * NC + ((c + (i & 1)) & 1)
        pick = onehot(iota((rows, 128), 1) == slot)
        cp_nxt.wait()
        values = jnp.broadcast_to(nxt[...].astype(F32), (128, 128)).T.astype(BF)
        values = jnp.concatenate([values, values], axis=1)[:, 0:three]
        expert_of = dot(pick, values).astype(jnp.int32)
        m2[...] = onehot(expert_of + experts * p == iota((rows, three), 1))

    def build_p4():
        j, i, p = split_jip(iota((1, rows), 1))
        source = ((x - (i >> 1)) & 3) * 96 + ((z - j) & 15) * 6 + ((c + (i & 1)) & 1) * 3 + p
        p4[...] = onehot(iota((rows, rows), 0) == source)
        cp_act.wait()
        cp_route.wait()

    def select(q):
        rb = route.shape[1]
        hit = jnp.where(route[q : q + 1, :] == iota((rb, rb), 0), 1.0, 0.0).astype(F32)
        picked = dot(hit.T.astype(BF), act_v[q * rb : (q + 1) * rb, :])
        alive = iota((rb, 1), 0) + q * rb < live[...]
        picked = jnp.where(alive, picked, 0.0).astype(BF)
        selp[q * rb : (q + 1) * rb, :] = dot(picked, p4[...]).astype(BF)

    pl.semaphore_wait(barrier, len(peers))

    def tell(r):
        for dz in (1 << r, NZ - (1 << r)):
            pl.semaphore_signal(tsem.at[r], inc=1, device_id=at(dz=dz), device_id_type=MESH)

    def hear(r):
        pl.semaphore_wait(tsem.at[r], 2)

    lo, hi = pl.ds(0, half), pl.ds(half, half)
    up, down = at(dy=1), at(dy=3)

    def r(k):
        all_of(gs.at[pl.ds(1, 3), k], lsem.at[k]).wait()
        remote(gs.at[2, k, lo], rel.at[k, 0], asend, arecv.at[0, k], up).start()
        remote(gs.at[2, k, hi], rel.at[k, 1], asend, arecv.at[0, k], down).start()

    def w(k):
        remote(gs.at[1, k, hi], parts_in.at[k, 0, hi], asend, arecv.at[1, k], up).start()
        remote(gs.at[3, k, lo], parts_in.at[k, 1, lo], asend, arecv.at[1, k], down).start()

    def a2(k):
        remote(rel.at[k], rel.at[k], asend, arecv.at[0, k], up).wait_recv()
        sums[k, 0] = (gs[1, k, 0:half].astype(F32) + rel[k, 0].astype(F32)).astype(BF)
        remote(sums.at[k, 0], parts_in.at[k, 0, lo], asend, arecv.at[1, k], up).start()
        sums[k, 1] = (gs[3, k, half:].astype(F32) + rel[k, 1].astype(F32)).astype(BF)
        remote(sums.at[k, 1], parts_in.at[k, 1, hi], asend, arecv.at[1, k], down).start()

    def exchange_z(s, k):
        for j in FAR_FIRST:
            remote(zsb.at[s, k, j], zrb.at[s, k, j], zsend, zrecv.at[s, k], at(dz=j)).start()

    def arrived_z(s, k):
        every = zrb.at[s, k, pl.ds(1, NZ - 1)]
        remote(every, every, zsend, zrecv.at[s, k], at(dz=1)).wait_recv()

    def exchange_s(s, k):
        for i in (4, 5, 2, 6, 3, 7, 1):
            remote(ssb.at[s, k, i], srb.at[s, k, i], ssend, srecv.at[s, k], at_i(i)).start()

    def arrived_s(s, k):
        every = srb.at[s, k, pl.ds(1, NS - 1)]
        remote(every, every, ssend, srecv.at[s, k], at_i(1)).wait_recv()

    def a3(k):
        remote(parts_in.at[k], parts_in.at[k], asend, arecv.at[1, k], up).wait_recv()
        if k == 0:
            all_of(gs.at[0], lsem.at[n]).wait()
        total = gs[0, k].astype(F32) + parts_in[k, 0].astype(F32) + parts_in[k, 1].astype(F32)
        moved = dot(p1[...], total.astype(BF)).reshape(NZ, 24, C).astype(BF)
        zsb[0, k] = moved
        zrb[0, k, 0] = moved[0]

    def zs(k):
        exchange_z(0, k)

    def b1(k):
        arrived_z(0, k)
        held = zrb[0, k].astype(F32).reshape(rows, C).astype(BF)
        moved = dot(p2[...], held).reshape(NS, 48, C).astype(BF)
        ssb[0, k] = moved
        srb[0, k, 0] = moved[0]
        exchange_s(0, k)

    def b2(k):
        arrived_s(0, k)
        totals = dot(m1[...], srb[0, k].reshape(rows, C))
        cols = slice(k * C, (k + 1) * C)
        new_momentum = momentum_decay * mom_v[:, :, cols].reshape(three, C) + totals
        nm_out[:, :, cols] = new_momentum.reshape(3, experts, C)
        master = mas_v[:, :, cols].reshape(three, C)
        weights = master - step_rate * new_momentum
        parts = []
        for b in range(C // QBLOCK):
            lanes_b = slice(b * QBLOCK, (b + 1) * QBLOCK)
            top = jnp.max(jnp.abs(master[:, lanes_b]), axis=1, keepdims=True)
            scale = (top / range_limit + epsilon).astype(BF).astype(F32)
            quantized = jnp.clip(weights[:, lanes_b] / scale, -range_limit, range_limit).astype(BF)
            parts.append((quantized.astype(F32) * scale).astype(BF))
        restored = parts[0] if len(parts) == 1 else jnp.concatenate(parts, axis=1)
        moved = dot(m2[...], restored).reshape(NS, 48, C).astype(BF)
        ssb[1, k] = moved
        srb[1, k, 0] = moved[0]
        exchange_s(1, k)

    def c1(k):
        arrived_s(1, k)
        moved = dot(p3[...], srb[1, k].reshape(rows, C)).reshape(NZ, 24, C).astype(BF)
        zsb[1, k] = moved
        zrb[1, k, 0] = moved[0]
        exchange_z(1, k)

    lo8, hi8 = pl.ds(0, NZ // 2), pl.ds(NZ // 2, NZ // 2)

    def d1(k):
        arrived_z(1, k)
        remote(zrb.at[1, k, lo8], wb.at[k, 0], dsend, drecv.at[0, k], up).start()
        remote(zrb.at[1, k, hi8], wb.at[k, 1], dsend, drecv.at[0, k], down).start()
        remote(zrb.at[1, k, hi8], wb.at[k, 2], dsend, drecv.at[1, k], up).start()
        remote(zrb.at[1, k, lo8], wb.at[k, 3], dsend, drecv.at[1, k], down).start()

    def multiply(k, held, b):
        weight = held.astype(F32).reshape(rows, C).astype(BF)
        off = pl.multiple_of(lax.rem(y + b, NY) * k_width + k * C, 128)
        out[:, pl.ds(off, C)] = dot(selp[...], weight).astype(BF)

    def halves(k, a, b):
        return jnp.concatenate([wb[k, a], wb[k, b]], axis=0)

    def arrived_d(k, which, first):
        pair = wb.at[k, pl.ds(first, 2)]
        remote(pair, pair, dsend, drecv.at[which, k], up).wait_recv()

    def d2(k):
        arrived_d(k, 0, 0)
        remote(wb.at[k, 0], wb.at[k, 4], dsend, drecv.at[2, k], up).start()
        remote(wb.at[k, 1], wb.at[k, 5], dsend, drecv.at[2, k], down).start()
        multiply(k, zrb[1, k], 0)

    def d3(k):
        arrived_d(k, 1, 2)
        multiply(k, halves(k, 0, 2), 3)
        multiply(k, halves(k, 3, 1), 1)
        arrived_d(k, 2, 4)
        multiply(k, halves(k, 4, 5), 2)

    r(0); w(0); tell(0); r(1); hear(0); tell(1); build_p1()
    a2(0); w(1); r(2); hear(1); tell(2); a2(1); w(2); r(3); a3(0); hear(2); zs(0)
    build_p2(); a2(2); w(3); a3(1); zs(1); build_m1(); a2(3); build_m2(); build_p3(); a3(2)
    cp_mom.wait()
    cp_mas.wait()
    zs(2); a3(3); build_p4(); b1(0); zs(3); select(0); select(1); b1(1); b2(0); b1(2); c1(0); b2(1); select(2); b1(3); b2(2); c1(1); select(3); b2(3); c1(2)
    d1(0); c1(3); d2(0); d1(1); d2(1); d3(0); d1(2); d2(2); d3(1); d1(3); d2(3); d3(2); d3(3)
    remote(gs.at[pl.ds(0, 3)], gs.at[pl.ds(0, 3)], asend, arecv.at[0, 0], up).wait_send()
    sent = zsb.at[:, :, pl.ds(1, NZ - 1)]
    remote(sent, sent, zsend, zrecv.at[0, 0], up).wait_send()
    sent = ssb.at[:, :, pl.ds(1, NS - 1)]
    remote(sent, sent, ssend, srecv.at[0, 0], up).wait_send()
    remote(wb, wb, dsend, drecv.at[0, 0], up).wait_send()


def deliver(nm_in, out_in, nm_out, out, sem):
    copies = [pltpu.make_async_copy(nm_in, nm_out, sem.at[0])]
    part = out.shape[0] // 4
    for q in range(4):
        piece = pl.ds(q * part, part)
        copies.append(pltpu.make_async_copy(out_in.at[piece], out.at[piece], sem.at[q + 1]))
    for cp in copies:
        cp.start()
    for cp in copies:
        cp.wait()


def shards(grads, momentum, master, current_slots, next_slots, live_counts, route_index, activations):
    grad = grads[0, 0]
    rows, width = grad.shape
    columns = momentum.shape[2]
    experts = momentum.shape[1]
    n = CHUNKS
    C = columns // n
    out_rows, hidden = activations.shape[2:]
    half = rows // 2
    hbm = pl.BlockSpec(memory_space=pltpu.MemorySpace.HBM)
    vmem = pl.BlockSpec(memory_space=pltpu.VMEM)

    def buf(*shape):
        return pltpu.VMEM(shape, BF)

    zbuf = buf(2, n, NZ, 24, C)
    sbuf = buf(2, n, NS, 48, C)
    sems = pltpu.SemaphoreType.DMA
    held = lambda a: pltpu.with_memory_space_constraint(a, pltpu.MemorySpace.HBM)
    new_momentum, expert_out = pl.pallas_call(
        functools.partial(kernel, C),
        out_shape=(
            jax.ShapeDtypeStruct(momentum.shape, F32),
            jax.ShapeDtypeStruct((out_rows, width), BF),
        ),
        in_specs=[hbm, hbm, hbm, hbm, hbm, vmem, hbm, hbm],
        out_specs=(vmem, vmem),
        scratch_shapes=[
            buf(NY, n, rows, C),
            pltpu.VMEM(momentum.shape, F32),
            pltpu.VMEM(momentum.shape, F32),
            buf(out_rows, hidden),
            pltpu.VMEM((1, current_slots.shape[0]), jnp.int32),
            pltpu.VMEM((1, current_slots.shape[0]), jnp.int32),
            pltpu.VMEM(route_index.shape[2:], jnp.int32),
            buf(n, 2, half, C), buf(n, 2, half, C), buf(n, 2, rows, C),
            zbuf, zbuf, sbuf, sbuf, buf(n, 6, NZ // 2, 24, C),
            buf(out_rows, hidden),
            buf(rows, rows), buf(rows, rows), buf(rows, rows), buf(rows, rows),
            buf(3 * experts, rows), buf(rows, 3 * experts),
            sems((n + 7,)),
            sems, sems((2, n)), sems, sems((2, n)), sems, sems((2, n)), sems, sems((3, n)),
            pltpu.SemaphoreType.REGULAR((3,)),
        ],
        compiler_params=pltpu.CompilerParams(
            collective_id=0, has_side_effects=True, vmem_limit_bytes=40 * 1024 * 1024
        ),
        name="step",
    )(
        held(grad), held(momentum), held(master), held(current_slots.reshape(1, -1)), held(next_slots.reshape(1, -1)), live_counts,
        held(route_index[0, 0]), held(activations[0, 0]),
    )
    new_momentum, expert_out = pl.pallas_call(
        deliver,
        out_shape=(
            jax.ShapeDtypeStruct(momentum.shape, F32),
            jax.ShapeDtypeStruct((out_rows, width), BF),
        ),
        in_specs=[vmem, vmem],
        out_specs=(hbm, hbm),
        scratch_shapes=[sems((5,))],
        compiler_params=pltpu.CompilerParams(vmem_limit_bytes=1024 * 1024),
        name="deliver",
    )(new_momentum, expert_out)
    return new_momentum, expert_out[None, None]


def solution(mesh):
    in_specs = (
        P("dp", "expert", None, None),
        P("expert", None, "dp"),
        P("expert", None, "dp"),
        P(),
        P(),
        P("dp", "expert"),
        P("dp", "expert", None, None),
        P("dp", "expert", None, None),
    )
    out_specs = (P("expert", None, "dp"), P("dp", "expert", None, None))
    return jax.shard_map(shards, mesh=mesh, in_specs=in_specs, out_specs=out_specs, check_vma=False)
```

time: 76.6 us -> 72.1 us (0.941)
  Pallas kernels: 72.4 us -> 69.8 us
  local copies, waits for them, and re-layouts: 2.07 us -> 0 us
    pallas_call x1, Pallas kernels: 72.4 us -> 68.3 us  [shards(): pl.pallas_call(functools.partial(kernel, C), out_shape=(jax.ShapeDtypeStr...]
    unnamed x2 -> x0, local copies, waits for them, and re-layouts: 2.07 us -> none
    pallas_call x0 -> x1, Pallas kernels: none -> 1.49 us  [shards(): pl.pallas_call(deliver, out_shape=(jax.ShapeDtypeStruct(momentum.shape, F...]
where the time goes in v3:
time: 72.1 us; the launch traced here: 71.1 us
  Pallas kernels  69.8 us (97%)
  between operations  1.29 us (2%)
    pallas_call x1, Pallas kernels, shards(): pl.pallas_call(functools.partial(kernel, C), out_shape=(jax.ShapeDtypeStr...  68.3 us
    pallas_call x1, Pallas kernels, shards(): pl.pallas_call(deliver, out_shape=(jax.ShapeDtypeStruct(momentum.shape, F...  1.49 us

profile of v3, /device:TPU:6, one launch (start us, length us, event | category | flops | bytes accessed | tf_op | source)
XLA Modules:
  0.0 71.1 jit_solution(9768558093597504073)
XLA Ops:
  1.3 68.3 %step.1 = (f32[3,64,512]{2,1,0:T(8,128)S(1)}, bf16[512,2048]{1,0:T(8,128)(2,1)S(1)}) custom-call(bf16[384,2048]{1,0:T(8,128)(2,1)} %bitcast.6, f32[3,64,512]{2,1,0:T(8,128)} %mom.1, f32[3,64,512]{2,1,0:T(8,128)} %mas.1, s32[1,128]{1,0:T(1,128)} %bitcast.9, s32[1,128]{1,0:T(1,128)} %bitcast.10, s32[1,1]{1,0:T(1,128)S(6)} %copy.10.live, s32[4,128]{1,0:T(4,128)} %bitcast.8, ...), custom_call_target="tpu_custom_call" | custom-call | tf_op jit(solution)/shard_map/step/pallas_call | solution.py:332
  69.6 1.5 %deliver.1 = (f32[3,64,512]{2,1,0:T(8,128)}, bf16[512,2048]{1,0:T(8,128)(2,1)}) custom-call(f32[3,64,512]{2,1,0:T(8,128)S(1)} %get-tuple-element.6.nm_in, bf16[512,2048]{1,0:T(8,128)(2,1)S(1)} %get-tuple-element.7.out_in), custom_call_target="tpu_custom_call" | custom-call | tf_op jit(solution)/shard_map/deliver/pallas_call | solution.py:365

commit v4 on v3

--- a/solution.py
+++ b/solution.py
@@ -91,18 +91,24 @@
         pl.semaphore_signal(barrier, inc=1, device_id=device, device_id_type=MESH)
 
     k_width = C * n
-    for k in range(n):
-        for b in (2, 1, 3):
-            off = pl.multiple_of(lax.rem(y + b, NY) * k_width + k * C, 128)
-            pltpu.make_async_copy(grad.at[:, pl.ds(off, C)], gs.at[b, k], lsem.at[k]).start()
-    for k in range(n):
-        off = pl.multiple_of(y * k_width + k * C, 128)
-        pltpu.make_async_copy(grad.at[:, pl.ds(off, C)], gs.at[0, k], lsem.at[n]).start()
+    def stage(k, b, sem):
+        off = pl.multiple_of(lax.rem(y + b, NY) * k_width + k * C, 128)
+        pltpu.make_async_copy(grad.at[:, pl.ds(off, C)], gs.at[b, k], lsem.at[sem]).start()
+
+    for b in (2, 1, 3):
+        stage(0, b, 0)
     small = [(act, act_v), (route_h, route), (cur_h, cur), (nxt_h, nxt), (mom, mom_v), (mas, mas_v)]
     small = [pltpu.make_async_copy(src, dst, lsem.at[n + 1 + at_]) for at_, (src, dst) in enumerate(small)]
     cp_act, cp_route, cp_cur, cp_nxt, cp_mom, cp_mas = small
-    for cp in (cp_cur, cp_nxt, cp_route, cp_act, cp_mom, cp_mas):
-        cp.start()
+
+    def stage_rest():
+        for k in range(1, n):
+            for b in (2, 1, 3):
+                stage(k, b, k)
+        for k in range(n):
+            stage(k, 0, n)
+        for cp in (cp_cur, cp_nxt, cp_route, cp_act, cp_mom, cp_mas):
+            cp.start()
 
     def all_of(ref, sem):
         return pltpu.make_async_copy(ref, ref, sem)
@@ -283,13 +289,13 @@
         arrived_d(k, 2, 4)
         multiply(k, halves(k, 4, 5), 2)
 
-    r(0); w(0); tell(0); r(1); hear(0); tell(1); build_p1()
+    r(0); w(0); tell(0); stage_rest(); r(1); hear(0); tell(1); build_p1()
     a2(0); w(1); r(2); hear(1); tell(2); a2(1); w(2); r(3); a3(0); hear(2); zs(0)
     build_p2(); a2(2); w(3); a3(1); zs(1); build_m1(); a2(3); build_m2(); build_p3(); a3(2)
     cp_mom.wait()
     cp_mas.wait()
     zs(2); a3(3); build_p4(); b1(0); zs(3); select(0); select(1); b1(1); b2(0); b1(2); c1(0); b2(1); select(2); b1(3); b2(2); c1(1); select(3); b2(3); c1(2)
-    d1(0); c1(3); d2(0); d1(1); d2(1); d3(0); d1(2); d2(2); d3(1); d1(3); d2(3); d3(2); d3(3)
+    d1(0); c1(3); d2(0); d1(1); d2(1); d1(2); d3(0); d2(2); d1(3); d3(1); d2(3); d3(2); d3(3)
     remote(gs.at[pl.ds(0, 3)], gs.at[pl.ds(0, 3)], asend, arecv.at[0, 0], up).wait_send()
     sent = zsb.at[:, :, pl.ds(1, NZ - 1)]
     remote(sent, sent, zsend, zrecv.at[0, 0], up).wait_send()
@@ -299,11 +305,7 @@
 
 
 def deliver(nm_in, out_in, nm_out, out, sem):
-    copies = [pltpu.make_async_copy(nm_in, nm_out, sem.at[0])]
-    part = out.shape[0] // 4
-    for q in range(4):
-        piece = pl.ds(q * part, part)
-        copies.append(pltpu.make_async_copy(out_in.at[piece], out.at[piece], sem.at[q + 1]))
+    copies = [pltpu.make_async_copy(out_in, out, sem.at[0]), pltpu.make_async_copy(nm_in, nm_out, sem.at[1])]
     for cp in copies:
         cp.start()
     for cp in copies:
@@ -370,7 +372,7 @@
         ),
         in_specs=[vmem, vmem],
         out_specs=(hbm, hbm),
-        scratch_shapes=[sems((5,))],
+        scratch_shapes=[sems((2,))],
         compiler_params=pltpu.CompilerParams(vmem_limit_bytes=1024 * 1024),
         name="deliver",
     )(new_momentum, expert_out)

time: 72.1 us -> 71.1 us (0.986)
  Pallas kernels: 69.8 us -> 68.9 us
    pallas_call x1, Pallas kernels: 68.3 us -> 67.4 us  [shards(): pl.pallas_call(functools.partial(kernel, C), out_shape=(jax.ShapeDtypeStr...]
where the time goes in v4:
time: 71.1 us; the launch traced here: 70.2 us
  Pallas kernels  68.9 us (97%)
  between operations  1.29 us (2%)
    pallas_call x1, Pallas kernels, shards(): pl.pallas_call(functools.partial(kernel, C), out_shape=(jax.ShapeDtypeStr...  67.4 us
    pallas_call x1, Pallas kernels, shards(): pl.pallas_call(deliver, out_shape=(jax.ShapeDtypeStruct(momentum.shape, F...  1.45 us

profile of v4, /device:TPU:6, one launch (start us, length us, event | category | flops | bytes accessed | tf_op | source)
XLA Modules:
  0.0 70.2 jit_solution(16651621777694491278)
XLA Ops:
  1.3 67.4 %step.1 = (f32[3,64,512]{2,1,0:T(8,128)S(1)}, bf16[512,2048]{1,0:T(8,128)(2,1)S(1)}) custom-call(bf16[384,2048]{1,0:T(8,128)(2,1)} %bitcast.6, f32[3,64,512]{2,1,0:T(8,128)} %mom.1, f32[3,64,512]{2,1,0:T(8,128)} %mas.1, s32[1,128]{1,0:T(1,128)} %bitcast.9, s32[1,128]{1,0:T(1,128)} %bitcast.10, s32[1,1]{1,0:T(1,128)S(6)} %copy.10.live, s32[4,128]{1,0:T(4,128)} %bitcast.8, ...), custom_call_target="tpu_custom_call" | custom-call | tf_op jit(solution)/shard_map/step/pallas_call | solution.py:334
  68.7 1.5 %deliver.1 = (f32[3,64,512]{2,1,0:T(8,128)}, bf16[512,2048]{1,0:T(8,128)(2,1)}) custom-call(f32[3,64,512]{2,1,0:T(8,128)S(1)} %get-tuple-element.6.nm_in, bf16[512,2048]{1,0:T(8,128)(2,1)S(1)} %get-tuple-element.7.out_in), custom_call_target="tpu_custom_call" | custom-call | tf_op jit(solution)/shard_map/deliver/pallas_call | solution.py:367

commit v5 on v4

--- a/solution.py
+++ b/solution.py
@@ -289,12 +289,13 @@
         arrived_d(k, 2, 4)
         multiply(k, halves(k, 4, 5), 2)
 
-    r(0); w(0); tell(0); stage_rest(); r(1); hear(0); tell(1); build_p1()
-    a2(0); w(1); r(2); hear(1); tell(2); a2(1); w(2); r(3); a3(0); hear(2); zs(0)
-    build_p2(); a2(2); w(3); a3(1); zs(1); build_m1(); a2(3); build_m2(); build_p3(); a3(2)
+    r(0); w(0); tell(0); stage_rest(); r(1); w(1); hear(0); tell(1); build_p1()
+    a2(0); r(2); w(2); hear(1); tell(2); a2(1); r(3); w(3); a3(0); hear(2); zs(0)
+    a2(2); a3(1); zs(1); a2(3); build_p2(); a3(2); zs(2); build_m1(); build_p3(); a3(3); zs(3); b1(0)
+    build_m2(); build_p4(); select(0)
     cp_mom.wait()
     cp_mas.wait()
-    zs(2); a3(3); build_p4(); b1(0); zs(3); select(0); select(1); b1(1); b2(0); b1(2); c1(0); b2(1); select(2); b1(3); b2(2); c1(1); select(3); b2(3); c1(2)
+    b1(1); b2(0); b1(2); select(1); c1(0); b2(1); b1(3); select(2); b2(2); c1(1); select(3); b2(3); c1(2)
     d1(0); c1(3); d2(0); d1(1); d2(1); d1(2); d3(0); d2(2); d1(3); d3(1); d2(3); d3(2); d3(3)
     remote(gs.at[pl.ds(0, 3)], gs.at[pl.ds(0, 3)], asend, arecv.at[0, 0], up).wait_send()
     sent = zsb.at[:, :, pl.ds(1, NZ - 1)]

time: 71.1 us -> 70.7 us (level); the launches traced: 70.2 us -> 70.6 us
  no operation moved by 1% of the time
where the time goes in v5:
time: 70.7 us; the launch traced here: 70.6 us
  Pallas kernels  69.3 us (98%)
  between operations  1.29 us (2%)
    pallas_call x1, Pallas kernels, shards(): pl.pallas_call(functools.partial(kernel, C), out_shape=(jax.ShapeDtypeStr...  67.8 us
    pallas_call x1, Pallas kernels, shards(): pl.pallas_call(deliver, out_shape=(jax.ShapeDtypeStruct(momentum.shape, F...  1.45 us

profile of v5, /device:TPU:6, one launch (start us, length us, event | category | flops | bytes accessed | tf_op | source)
XLA Modules:
  0.0 70.6 jit_solution(18158682080797353785)
XLA Ops:
  1.3 67.8 %step.1 = (f32[3,64,512]{2,1,0:T(8,128)S(1)}, bf16[512,2048]{1,0:T(8,128)(2,1)S(1)}) custom-call(bf16[384,2048]{1,0:T(8,128)(2,1)} %bitcast.6, f32[3,64,512]{2,1,0:T(8,128)} %mom.1, f32[3,64,512]{2,1,0:T(8,128)} %mas.1, s32[1,128]{1,0:T(1,128)} %bitcast.9, s32[1,128]{1,0:T(1,128)} %bitcast.10, s32[1,1]{1,0:T(1,128)S(6)} %copy.10.live, s32[4,128]{1,0:T(4,128)} %bitcast.8, ...), custom_call_target="tpu_custom_call" | custom-call | tf_op jit(solution)/shard_map/step/pallas_call | solution.py:335
  69.1 1.5 %deliver.1 = (f32[3,64,512]{2,1,0:T(8,128)}, bf16[512,2048]{1,0:T(8,128)(2,1)}) custom-call(f32[3,64,512]{2,1,0:T(8,128)S(1)} %get-tuple-element.6.nm_in, bf16[512,2048]{1,0:T(8,128)(2,1)S(1)} %get-tuple-element.7.out_in), custom_call_target="tpu_custom_call" | custom-call | tf_op jit(solution)/shard_map/deliver/pallas_call | solution.py:368
